TPU v7x, 32 devices: a whole 2x2x4 slice. The times are simulated.
32 devices in a mesh: dp: 8 (over z, x), tp: 4 (over y, core).
Axes of the slice: x: 2, y: 2, z: 4, core: 2. Of those that a mesh axis runs over, the one named last changes fastest.
Arguments:
- activations: bfloat16 [2048, 4096], P(('dp', 'tp')), may hold values from -700 to 700
- cotangent: bfloat16 [2048, 512], P('dp', 'tp'), may hold values from -6 to 6
- segment_ids: int32 [2048], P('dp'), may hold values from 0 to 31, never falling along the last dimension, each value on 1 to 128 neighbouring positions
- norm_gain: float32 [4096], replicated, may hold values from 0.5 to 1.5
- query_weight: bfloat16 [4096, 512], P(None, 'tp'), may hold values from -2 to 2
- key_value_weight: bfloat16 [4096, 512], P(None, 'tp'), may hold values from -1 to 1
Outputs:
- input_grad: bfloat16 [2048, 4096], P(('dp', 'tp'))
- query_grad: bfloat16 [4096, 512], P(None, 'tp')
- key_value_grad: bfloat16 [4096, 512], P(None, 'tp')
- gain_grad: float32 [4096], replicated
Inputs may be any that keep to these rules, and one draw needn't show every extreme that they name: `segment_ids`: document numbers never fall along the tokens; a document has 1 to 128 tokens and may run on from one replica's rows into the next.
All inputs are finite; a program needn't handle non-finite values.
Results may differ from a plain program's by a relative error of at most 0.03.
Values may be sent and summed in bfloat16 or wider, within the bound.
A program may use at most 64 MiB of HBM per device.

v0:
```python
import jax
import jax.numpy as jnp
from jax import lax
from jax.sharding import PartitionSpec as P

EPS = 1e-05


def swapped(value, axis, bit):
    mask = 2**bit
    pairs = [(source, source ^ mask) for source in range(lax.axis_size(axis))]
    return lax.ppermute(value, axis, pairs)


def rope_tables(length, width):
    position = jnp.arange(length, dtype=jnp.float32)
    frequency = 500000.0 ** (-jnp.arange(0, width, 2, dtype=jnp.float32) / width)
    angle = position[:, None] * frequency[None, :]
    return (jnp.cos(angle), jnp.sin(angle))


def rotate(values, cosine, sine):
    half = values.shape[1] // 2
    first = values[:, :half]
    second = values[:, half:]
    return jnp.concatenate([first * cosine - second * sine, second * cosine + first * sine], axis=1)


def contract_rows(left, right):
    return lax.dot_general(
        left, right, (((0,), (0,)), ((), ())), preferred_element_type=jnp.float32
    )


def times_transposed(left, right):
    return lax.dot_general(
        left, right, (((1,), (1,)), ((), ())), preferred_element_type=jnp.float32
    )


def on_device(activations, cotangent, segment_ids, norm_gain, query_weight, key_value_weight):
    width = query_weight.shape[1]
    scale = width ** (-0.5)
    inputs_f = activations.astype(jnp.float32)
    root_mean = jnp.sqrt(jnp.mean(inputs_f * inputs_f, axis=1, keepdims=True) + EPS)
    unit_rows = inputs_f / root_mean
    normed_local = (unit_rows * norm_gain[None, :]).astype(jnp.bfloat16)
    normed = lax.all_gather(normed_local, "tp", axis=0, tiled=True)
    length = normed.shape[0]
    cosine, sine = rope_tables(length, width)
    holds_value = lax.axis_index("tp") % 2 == 1
    query_raw = jnp.dot(normed, query_weight, preferred_element_type=jnp.float32)
    query = rotate(query_raw, cosine, sine).astype(jnp.bfloat16)
    projected = jnp.dot(normed, key_value_weight, preferred_element_type=jnp.float32)
    own_rows = jnp.where(holds_value, projected, rotate(projected, cosine, sine)).astype(
        jnp.bfloat16
    )
    partner_rows = swapped(own_rows, "tp", 0)
    keys = jnp.where(holds_value, partner_rows, own_rows)
    values = jnp.where(holds_value, own_rows, partner_rows)
    position = jnp.arange(length)
    allowed = (position[:, None] >= position[None, :]) & (
        segment_ids[:, None] == segment_ids[None, :]
    )
    scores = jnp.where(allowed, times_transposed(query, keys) * scale, jnp.float32(-1e30))
    top = jnp.max(scores, axis=1, keepdims=True)
    exp_scores = jnp.exp(scores - top)
    probs = exp_scores / jnp.sum(exp_scores, axis=1, keepdims=True)
    probs_half = probs.astype(jnp.bfloat16)
    prob_grad = times_transposed(cotangent, values)
    delta = jnp.sum(probs * prob_grad, axis=1, keepdims=True)
    score_grad = (probs * (prob_grad - delta) * scale).astype(jnp.bfloat16)
    query_part = rotate(
        jnp.dot(score_grad, keys, preferred_element_type=jnp.float32), cosine, -sine
    ).astype(jnp.bfloat16)
    key_part = rotate(contract_rows(score_grad, query), cosine, -sine).astype(jnp.bfloat16)
    value_part = contract_rows(probs_half, cotangent).astype(jnp.bfloat16)
    query_term = contract_rows(normed, query_part)
    own_grad = jnp.where(holds_value, value_part, key_part)
    outgoing = jnp.where(holds_value, key_part, value_part)
    incoming = swapped(outgoing, "tp", 0)
    pair_term = contract_rows(normed, own_grad) + contract_rows(normed, incoming)
    total = times_transposed(query_part, query_weight)
    total = total + times_transposed(own_grad, key_value_weight)
    normed_grad = lax.psum_scatter(
        (total + times_transposed(incoming, key_value_weight)).astype(jnp.bfloat16),
        "tp",
        scatter_dimension=0,
        tiled=True,
    ).astype(jnp.float32)
    summed = (
        lax.psum(query_term.astype(jnp.bfloat16), "dp").astype(jnp.float32),
        lax.psum(pair_term.astype(jnp.bfloat16), "dp").astype(jnp.float32),
    )
    gain_term = jnp.sum(normed_grad * unit_rows, axis=0)
    gain_grad = lax.psum(gain_term, ("dp", "tp"))
    scaled = normed_grad * norm_gain[None, :]
    inner = jnp.mean(scaled * unit_rows, axis=1, keepdims=True)
    input_grad = ((scaled - unit_rows * inner) / root_mean).astype(jnp.bfloat16)
    return (input_grad, summed[0].astype(jnp.bfloat16), summed[1].astype(jnp.bfloat16), gain_grad)


def solution(mesh):
    return jax.shard_map(
        on_device,
        mesh=mesh,
        in_specs=(P(("dp", "tp"), None), P("dp", "tp"), P("dp"), P(), P(None, "tp"), P(None, "tp")),
        out_specs=(P(("dp", "tp"), None), P(None, "tp"), P(None, "tp"), P()),
        check_vma=False,
    )
```

profile of v0, /device:TPU:0, one launch (start us, length us, event | category | flops | bytes accessed | tf_op | source)
XLA Modules:
  0.0 196.8 jit_solution(11558422699081781920)
XLA Ops:
  7.2 1.3 fusion.8
  8.6 2.1 %multiply_convert_fusion = bf16[64,4096]{1,0:T(8,128)(2,1)} fusion(f32[4096]{0:T(1024)} %param.9, f32[64]{0:T(128)S(1)} %add_sqrt_fusion, bf16[64,4096]{1,0:T(8,128)(2,1)} %param.6), kind=kLoop, calls=%fused_computation.21 | loop fusion | flops 1048576 | bytes 1065216 | tf_op jit(solution)/shard_map/convert_element_type | solution.py:47
  10.7 25.4 %all-gather.2.cloned.1.call-done = bf16[256,4096]{1,0:T(8,128)(2,1)} async-done(((bf16[64,4096]{1,0:T(8,128)(2,1)}), bf16[256,4096]{1,0:T(8,128)(2,1)}) %all-gather.2.cloned.1.call-update) | async-done | bytes 2097168 | tf_op jit(solution)/shard_map/all_gather | solution.py:48
  36.1 2.6 %fusion.33 = f32[256,128]{0,1:T(8,128)S(1)} fusion(bf16[256,4096]{1,0:T(8,128)(2,1)} %all-gather.2.cloned.1.call-done, bf16[4096,128]{1,0:T(8,128)(2,1)S(1)} %copy-done), kind=kOutput, calls=%fused_computation.67 | convolution fusion | flops 268435456 | bytes 3276800 | tf_op jit(solution)/shard_map/dot_general | solution.py:54
  38.7 0.3 multiply_subtract_fusion
  39.0 0.3 collective-permute-start
  39.4 2.0 %fusion.32 = f32[256,128]{0,1:T(8,128)S(1)} fusion(bf16[256,4096]{1,0:T(8,128)(2,1)S(1)} %copy-done.1, bf16[4096,128]{1,0:T(8,128)(2,1)} %param.10), kind=kOutput, calls=%fused_computation.66 | convolution fusion | flops 268435456 | bytes 3276800 | tf_op jit(solution)/shard_map/dot_general | solution.py:52
  41.4 0.3 subtract_convert_fusion.2
  41.8 0.3 fusion.31
  42.8 0.3 subtract_convert_fusion
  43.4 0.3 collective-permute-start.1
  43.7 0.7 fusion.20
  44.5 0.7 convolution_add_fusion.1
  45.2 2.1 %fusion = bf16[256,4096]{1,0:T(8,128)(2,1)} fusion(f32[256,4096]{1,0:T(8,128)S(1)} %convolution_add_fusion.1, bf16[256,128]{0,1:T(8,128)(2,1)S(1)} %collective-permute-done.1, bf16[4096,128]{1,0:T(8,128)(2,1)S(1)} %copy-done), kind=kOutput, calls=%fused_computation.2 | convolution fusion | flops 270532608 | bytes 7405568 | tf_op jit(solution)/shard_map/dot_general | solution.py:36
  47.4 1.7 convolution_convert_fusion
  49.1 0.8 fusion.23
  49.9 1.8 fusion.1
  51.7 27.2 %reduce-scatter.2.cloned.1.call-done = bf16[64,4096]{1,0:T(8,128)(2,1)} async-done(((bf16[256,4096]{1,0:T(8,128)(2,1)}), bf16[64,4096]{1,0:T(8,128)(2,1)}) %reduce-scatter.2.cloned.1.call-update) | async-done | bytes 524304 | tf_op jit(solution)/shard_map/reduce_scatter | solution.py:85
  78.9 1.5 fusion.9
  80.4 42.6 %psum.23 = f32[4096]{0:T(1024)} all-reduce(f32[4096]{0:T(1024)S(1)} %get-tuple-element.4), channel_id=1, replica_groups=mesh['dp'=8,'tp'=4] {'dp','tp'}, use_global_device_ids=true, to_apply=%region_9.10 | all-reduce | flops 4096 | bytes 32768 | tf_op jit(solution)/shard_map/psum | solution.py:96
  123.0 2.1 %fusion.7 = bf16[64,4096]{1,0:T(8,128)(2,1)} fusion(bf16[64,4096]{1,0:T(8,128)(2,1)} %reduce-scatter.2.cloned.1.call-done, f32[64]{0:T(128)S(1)} %broadcast_multiply_fusion, f32[4096]{0:T(1024)S(1)} %copy-done.5, f32[64]{0:T(128)S(1)} %add_sqrt_fusion, bf16[64,4096]{1,0:T(8,128)(2,1)S(1)} %copy-done.2), kind=kLoop, calls=%fused_computation.18 | loop fusion | flops 2097152 | bytes 1589760 | tf_op jit(solution)/shard_map/convert_element_type | solution.py:99
  125.2 61.8 %all-reduce.3.cloned.1.call-done = (bf16[4096,128]{1,0:T(8,128)(2,1)}, bf16[4096,128]{1,0:T(8,128)(2,1)}) async-done(((bf16[4096,128]{1,0:T(8,128)(2,1)}, bf16[4096,128]{1,0:T(8,128)(2,1)}), (bf16[4096,128]{1,0:T(8,128)(2,1)}, bf16[4096,128]{1,0:T(8,128)(2,1)})) %all-reduce.3.cloned.1.call-update) | async-done | bytes 2097168 | tf_op jit(solution)/shard_map/psum | solution.py:92
  186.9 2.4 %copy.14 = bf16[4096,128]{1,0:T(8,128)(2,1)} copy(bf16[4096,128]{1,0:T(8,128)(2,1)} %get-tuple-element.25) | data formatting | bytes 2097152
  189.3 1.0 copy.15
  (34 shorter events, 1.2 us)
Async XLA Ops:
  7.2 28.9 %copy-start = (bf16[4096,128]{1,0:T(8,128)(2,1)S(1)}, bf16[4096,128]{1,0:T(8,128)(2,1)}, u32[]{:S(2)}) copy-start(bf16[4096,128]{1,0:T(8,128)(2,1)} %param.11) | copy-start | bytes 3145732
  7.2 28.9 %all-gather.2.cloned.1.call-start = ((), (), s32[]{:S(2)}) async-start(), calls=%async_computation.1 | async-start | bytes 2621440 | tf_op jit(solution)/shard_map/all_gather | solution.py:48
  10.7 68.3 %reduce-scatter.2.cloned.1.call-start = ((), (), s32[]{:S(2)}) async-start(), calls=%async_computation.2 | async-start | bytes 2621440 | tf_op jit(solution)/shard_map/reduce_scatter | solution.py:85
  36.1 3.3 %copy-start.1 = (bf16[256,4096]{1,0:T(8,128)(2,1)S(1)}, bf16[256,4096]{1,0:T(8,128)(2,1)}, u32[]{:S(2)}) copy-start(bf16[256,4096]{1,0:T(8,128)(2,1)} %all-gather.2.cloned.1.call-done) | copy-start | bytes 6291460
  38.7 3.1 %copy-start.7 = (s32[256]{0:T(256)S(1)}, s32[256]{0:T(256)}, u32[]{:S(2)}) copy-start(s32[256]{0:T(256)} %param.8) | copy-start | bytes 3076
  39.0 3.1 %copy-start.6 = (bf16[256,128]{1,0:T(8,128)(2,1)S(1)}, bf16[256,128]{1,0:T(8,128)(2,1)}, u32[]{:S(2)}) copy-start(bf16[256,128]{1,0:T(8,128)(2,1)} %param.7) | copy-start | bytes 196612
  39.0 2.7 %collective-permute-start = (bf16[256,128]{0,1:T(8,128)(2,1)S(1)}, bf16[256,128]{0,1:T(8,128)(2,1)S(1)}, u32[]{:S(2)}, u32[]{:S(2)}) collective-permute-start(bf16[256,128]{0,1:T(8,128)(2,1)S(1)} %fusion.13), channel_id=1, source_target_pairs={{0,1},{1,0},{2,3},{3,2},{4,5},{5,4},{6,7},{7,6},{8,9},{9,8},{10,11... | collective-permute-start | bytes 196616 | tf_op jit(solution)/shard_map/ppermute | solution.py:12
  42.1 1.6 copy-start.3
  43.4 1.8 collective-permute-start.1
  47.3 139.6 %all-reduce.3.cloned.1.call-start = ((), (), s32[]{:S(2)}) async-start(), calls=%async_computation.3 | async-start | bytes 4194304 | tf_op jit(solution)/shard_map/psum | solution.py:92
  51.7 27.3 %copy-start.2 = (bf16[64,4096]{1,0:T(8,128)(2,1)S(1)}, bf16[64,4096]{1,0:T(8,128)(2,1)}, u32[]{:S(2)}) copy-start(bf16[64,4096]{1,0:T(8,128)(2,1)} %param.6) | copy-start | bytes 1572868
  51.7 27.3 %copy-start.5 = (f32[4096]{0:T(1024)S(1)}, f32[4096]{0:T(1024)}, u32[]{:S(2)}) copy-start(f32[4096]{0:T(1024)} %param.9) | copy-start | bytes 49156
  186.9 2.4 %copy-start.4 = (bf16[4096,128]{1,0:T(8,128)(2,1)S(1)}, bf16[4096,128]{1,0:T(8,128)(2,1)}, u32[]{:S(2)}) copy-start(bf16[4096,128]{1,0:T(8,128)(2,1)} %get-tuple-element.26) | copy-start | bytes 3145732
Sparse Core Ops, SparseCore 0:
  10.8 25.2 all-gather.1
  47.5 31.4 reduce-scatter.1
  83.6 103.2 all-reduce.2
where the time goes:
time: 197 us
  waiting for transfers between devices  114 us (58%)
  blocking collectives  42.6 us (22%)
  between operations  13.9 us (7%)
  matrix products  13.5 us (7%)
  other arithmetic  8.2 us (4%)
  local copies, waits for them, and re-layouts  3.36 us (2%)
    psum x1, waiting for transfers between devices, on_device(): lax.psum(query_term.astype(jnp.bfloat16), 'dp').astype(jnp.float32)  61.8 us
    psum x1, blocking collectives, on_device(): gain_grad = lax.psum(gain_term, ('dp', 'tp'))  42.6 us
    reduce_scatter x1, waiting for transfers between devices, on_device(): lax.psum_scatter((total + times_transposed(incoming, key_value_weight)).a...  27.2 us
    all_gather x1, waiting for transfers between devices, on_device(): normed = lax.all_gather(normed_local, 'tp', axis=0, tiled=True)  25.4 us
    dot_general x5, matrix products, contract_rows(): lax.dot_general(left, right, (((0,), (0,)), ((), ())), preferred_element_...  4.68 us
    dot_general x5, matrix products, times_transposed(): lax.dot_general(left, right, (((1,), (1,)), ((), ())), preferred_element_...  4.08 us
  transfers between devices with their start and end apart: 5, of which 3 were waited for; matrix products, arithmetic and copies ran while one was open for 6% of the time, Pallas kernels for 0%

commit v1 on v0

v1 whole, which is shorter than its diff:
```python
import functools

import jax
import jax.numpy as jnp
import numpy as np
from jax import lax
from jax.experimental import pallas as pl
from jax.experimental.pallas import tpu as pltpu
from jax.sharding import PartitionSpec as P

EPS = 1e-05
AG_CHUNKS = 4
DP_CHUNKS = 4
RS_CHUNKS = 4


def low_bit(d):
    return d & -d


def bits_of(n):
    return [1 << k for k in range(n.bit_length() - 1)]


def bit_at(v, b):
    return lax.rem(lax.div(v, b), 2)


def xor(v, mask):
    out = v
    for b in bits_of(1 << mask.bit_length()):
        if mask & b:
            out = out + b - 2 * b * bit_at(v, b)
    return out


def dot(a, b, ca, cb):
    return lax.dot_general(a, b, (((ca,), (cb,)), ((), ())), preferred_element_type=jnp.float32)


def kernel(ntp, ndp, x_ref, cot_ref, seg_ref, gain_ref, cos_ref, sin_ref, wq_ref, wkv_ref,
           ig_ref, qg_ref, kvg_ref, gg_ref,
           wcat, normed, grads, tot, rs_out, rs_in, term, halves, whole, gs, gr, kv_out, kv_in, inv_ref,
           w_sem, o_sem, ag_s, ag_r, rs_s, rs_r, dp_s, dp_r, g_s, g_r, kv_s, kv_r):
    tp, dp = lax.axis_index("tp"), lax.axis_index("dp")
    tp_bits, dp_bits = bits_of(ntp), bits_of(ndp)
    rows, width = x_ref.shape
    length = cot_ref.shape[0]
    head = cot_ref.shape[1]
    sends = []

    def remote(src, dst, s, r, axis, b):
        me = tp if axis == "tp" else dp
        return pltpu.make_async_remote_copy(
            src_ref=src, dst_ref=dst, send_sem=s, recv_sem=r,
            device_id={axis: xor(me, b)}, device_id_type=pl.DeviceIdType.MESH)

    def go(copy):
        copy.start()
        sends.append(copy)

    barrier = pltpu.get_barrier_semaphore()
    for b in tp_bits:
        pl.semaphore_signal(barrier, inc=1, device_id={"tp": xor(tp, b)},
                            device_id_type=pl.DeviceIdType.MESH)
    for b in dp_bits:
        pl.semaphore_signal(barrier, inc=1, device_id={"dp": xor(dp, b)},
                            device_id_type=pl.DeviceIdType.MESH)

    w_copies = [pltpu.make_async_copy(wq_ref, wcat.at[:, 0:head], w_sem.at[0]),
                pltpu.make_async_copy(wkv_ref, wcat.at[:, head:2 * head], w_sem.at[1])]
    for copy in w_copies:
        copy.start()

    def block(d):
        return pl.ds(pl.multiple_of(xor(tp, d) * rows, rows), rows)

    cw = width // AG_CHUNKS

    def cols(c, w=cw):
        return slice(c * w, (c + 1) * w)

    square = jnp.zeros((rows, 1), jnp.float32)
    for c in range(AG_CHUNKS):
        v = x_ref[:, cols(c)].astype(jnp.float32)
        square = square + jnp.sum(v * v, axis=1, keepdims=True)
    inv = 1.0 / jnp.sqrt(square * (1.0 / width) + EPS)
    inv_ref[...] = jnp.broadcast_to(inv, inv_ref.shape)

    def ag(c, d):
        b = low_bit(d)
        part = normed.at[block(d ^ b), cols(c)]
        return remote(part, part, ag_s.at[c, d], ag_r.at[c, d], "tp", b)

    order = sorted(range(1, ntp), key=lambda d: -low_bit(d))
    for c in range(AG_CHUNKS):
        unit = x_ref[:, cols(c)].astype(jnp.float32) * inv
        normed[block(0), cols(c)] = (unit * gain_ref[:, cols(c)]).astype(jnp.bfloat16)
        if c == 0:
            pl.semaphore_wait(barrier, len(tp_bits) + len(dp_bits))
        for b in reversed(tp_bits):
            go(ag(c, b))
    for copy in w_copies:
        copy.wait()
    proj = jnp.zeros((length, 2 * head), jnp.float32)

    def forward(c):
        for d in order:
            if low_bit(d) > 1:
                ag(c, d).wait_recv()
                for b in reversed(tp_bits):
                    if b < low_bit(d):
                        go(ag(c, d | b))

    def arrive(c, proj):
        for d in order:
            if low_bit(d) == 1:
                ag(c, d).wait_recv()
        return proj + dot(normed[:, cols(c)], wcat[cols(c), :], 1, 0)

    forward(0)
    for c in range(AG_CHUNKS):
        if c + 1 < AG_CHUNKS:
            forward(c + 1)
        proj = arrive(c, proj)

    odd = lax.rem(tp, 2) == 1
    cosine, sine = cos_ref[...], sin_ref[...]

    def rope(u):
        return u * cosine + pltpu.roll(u, head // 2, 1) * sine

    def rope_t(u):
        return u * cosine - pltpu.roll(u, head // 2, 1) * sine

    raw = proj[:, head:]
    own = jnp.where(odd, raw, rope(raw))
    kv_out[0] = own.astype(jnp.bfloat16)
    swap = remote(kv_out.at[0], kv_in.at[0], kv_s.at[0], kv_r.at[0], "tp", 1)
    go(swap)
    query = rope(proj[:, :head]).astype(jnp.bfloat16)
    seg_s = jnp.broadcast_to(seg_ref[...].astype(jnp.float32), (length, length))
    seg_t = seg_s.T
    t_at = lax.broadcasted_iota(jnp.int32, (length, length), 0)
    s_at = lax.broadcasted_iota(jnp.int32, (length, length), 1)
    allowed = (t_at >= s_at) & (seg_s == seg_t)
    scale = head ** (-0.5)
    swap.wait_recv()
    mine, other = kv_out[0].astype(jnp.float32), kv_in[0].astype(jnp.float32)
    keys = jnp.where(odd, other, mine).astype(jnp.bfloat16)
    values = jnp.where(odd, mine, other).astype(jnp.bfloat16)
    cot = cot_ref[...]
    scores = jnp.where(allowed, dot(query, keys, 1, 1) * scale, jnp.float32(-1e30))
    top = jnp.max(scores, axis=1, keepdims=True)
    e = jnp.exp(scores - top)
    probs = e / jnp.sum(e, axis=1, keepdims=True)
    prob_grad = dot(cot, values, 1, 1)
    delta = jnp.sum(probs * prob_grad, axis=1, keepdims=True)
    score_grad = (probs * (prob_grad - delta) * scale).astype(jnp.bfloat16)
    key_part = rope_t(dot(score_grad, query, 0, 0))
    value_part = dot(probs.astype(jnp.bfloat16), cot, 0, 0)
    kv_out[1] = jnp.where(odd, key_part, value_part).astype(jnp.bfloat16)
    swap = remote(kv_out.at[1], kv_in.at[1], kv_s.at[1], kv_r.at[1], "tp", 1)
    go(swap)
    own_grad = jnp.where(odd, value_part, key_part).astype(jnp.bfloat16).astype(jnp.float32)
    grads[:, :head] = rope_t(dot(score_grad, keys, 1, 0)).astype(jnp.bfloat16)
    swap.wait_recv()
    grads[:, head:] = (own_grad + kv_in[1].astype(jnp.float32)).astype(jnp.bfloat16)

    local = []

    def dp_task(q):
        bits = dp_bits if q % 2 == 0 else dp_bits[1:] + dp_bits[:1]
        nb = len(bits)
        size = width // DP_CHUNKS
        term[cols(q, size), :] = dot(normed[:, cols(q, size)], grads[...], 0, 0).astype(jnp.bfloat16)
        start, count, offset = q * size, size, 0
        starts = []
        copies = []
        for k, b in enumerate(bits):
            count = count // 2
            up = bit_at(dp, b)
            starts.append(start)
            away = pl.multiple_of(start + (1 - up) * count, count)
            keep = pl.multiple_of(start + up * count, count)
            land = halves.at[q, pl.ds(offset, count), :]
            copy = remote(term.at[pl.ds(away, count), :], land, dp_s.at[q, k], dp_r.at[q, k], "dp", b)
            go(copy)
            yield
            copy.wait_recv()
            summed = (term[pl.ds(keep, count), :].astype(jnp.float32)
                      + halves[q, pl.ds(offset, count), :].astype(jnp.float32)).astype(jnp.bfloat16)
            if k + 1 < nb:
                term[pl.ds(keep, count), :] = summed
            else:
                whole[pl.ds(keep, count), :] = summed
            start, offset = keep, offset + count
        for k in reversed(range(nb)):
            part = whole.at[pl.ds(start, count), :]
            copy = remote(part, part, dp_s.at[q, nb + k], dp_r.at[q, nb + k], "dp", bits[k])
            go(copy)
            yield
            copy.wait_recv()
            start, count = starts[k], count * 2
        for i, out in enumerate((qg_ref, kvg_ref)):
            copy = pltpu.make_async_copy(
                whole.at[cols(q, size), i * head:(i + 1) * head], out.at[cols(q, size), :], o_sem.at[q, i])
            copy.start()
            local.append(copy)

    rw = width // RS_CHUNKS
    rs_order = sorted(range(1, ntp), key=low_bit)

    def rs(c, d):
        return remote(rs_out.at[d, :, cols(c, rw)], rs_in.at[d, :, cols(c, rw)],
                      rs_s.at[c, d], rs_r.at[c, d], "tp", low_bit(d))

    def partial(c, d):
        value = tot[block(d), cols(c, rw)]
        for b in tp_bits:
            if d == 0 or b < low_bit(d):
                value = value + rs_in[d | b, :, cols(c, rw)].astype(jnp.float32)
        return value

    def rs_send(c, b):
        for d in rs_order:
            if low_bit(d) == b:
                rs_out[d, :, cols(c, rw)] = partial(c, d).astype(jnp.bfloat16)
                go(rs(c, d))

    def rs_wait(c, b):
        for d in rs_order:
            if low_bit(d) == b:
                rs(c, d).wait_recv()

    def tp_task():
        for c in range(RS_CHUNKS):
            tot[:, cols(c, rw)] = dot(grads[...], wcat[cols(c, rw), :], 1, 1)
            rs_send(c, 1)
        for b in tp_bits[1:]:
            for c in range(RS_CHUNKS):
                rs_wait(c, b // 2)
                rs_send(c, b)
        yield
        inner = jnp.zeros((rows, 1), jnp.float32)
        scale_back = inv_ref[:, 0:1]
        for c in range(RS_CHUNKS):
            rs_wait(c, tp_bits[-1])
            value = partial(c, 0)
            tot[block(0), cols(c, rw)] = value
            product = value * (x_ref[:, cols(c, rw)].astype(jnp.float32) * scale_back)
            gs[0, :, cols(c, rw)] = jnp.sum(product, axis=0, keepdims=True)
            inner = inner + jnp.sum(product * gain_ref[:, cols(c, rw)], axis=1, keepdims=True)
        rounds = [("tp", b) for b in tp_bits] + [("dp", b) for b in dp_bits]

        def exchange(k):
            axis, b = rounds[k]
            return remote(gs.at[k], gr.at[k], g_s.at[k], g_r.at[k], axis, b)

        go(exchange(0))
        inner = inner * (1.0 / width)
        for c in range(RS_CHUNKS):
            unit = x_ref[:, cols(c, rw)].astype(jnp.float32) * scale_back
            scaled = tot[block(0), cols(c, rw)] * gain_ref[:, cols(c, rw)]
            ig_ref[:, cols(c, rw)] = ((scaled - unit * inner) * scale_back).astype(jnp.bfloat16)
        for k in range(len(rounds)):
            yield
            exchange(k).wait_recv()
            if k + 1 < len(rounds):
                gs[k + 1] = gs[k] + gr[k]
                go(exchange(k + 1))
            else:
                gg_ref[...] = gs[k] + gr[k]

    tasks = [dp_task(q) for q in range(DP_CHUNKS)] + [tp_task()]
    while tasks:
        alive = []
        for task in tasks:
            try:
                next(task)
                alive.append(task)
            except StopIteration:
                pass
        tasks = alive
    for copy in local:
        copy.wait()
    for copy in sends:
        copy.wait_send()


def on_device(ntp, ndp, activations, cotangent, segment_ids, norm_gain, query_weight, key_value_weight):
    rows, width = activations.shape
    length, head = cotangent.shape
    angle = np.arange(length)[:, None] * 500000.0 ** (-np.arange(0, head, 2) / head)[None, :]
    cosine = np.concatenate([np.cos(angle), np.cos(angle)], axis=1).astype(np.float32)
    sine = np.concatenate([-np.sin(angle), np.sin(angle)], axis=1).astype(np.float32)
    nb = len(bits_of(ntp)) + len(bits_of(ndp))
    bf, f32 = jnp.bfloat16, jnp.float32
    vmem = pl.BlockSpec(memory_space=pltpu.VMEM)
    anywhere = pl.BlockSpec(memory_space=pl.ANY)
    dma = pltpu.SemaphoreType.DMA
    nd = len(bits_of(ndp))
    outs = pl.pallas_call(
        functools.partial(kernel, ntp, ndp),
        out_shape=[
            jax.ShapeDtypeStruct((rows, width), bf),
            jax.ShapeDtypeStruct((width, head), bf),
            jax.ShapeDtypeStruct((width, head), bf),
            jax.ShapeDtypeStruct((1, width), f32),
        ],
        in_specs=[vmem] * 6 + [anywhere] * 2,
        out_specs=[vmem, anywhere, anywhere, vmem],
        scratch_shapes=[
            pltpu.VMEM((width, 2 * head), bf),
            pltpu.VMEM((length, width), bf),
            pltpu.VMEM((length, 2 * head), bf),
            pltpu.VMEM((length, width), f32),
            pltpu.VMEM((ntp, rows, width), bf),
            pltpu.VMEM((ntp, rows, width), bf),
            pltpu.VMEM((width, 2 * head), bf),
            pltpu.VMEM((DP_CHUNKS, width // DP_CHUNKS, 2 * head), bf),
            pltpu.VMEM((width, 2 * head), bf),
            pltpu.VMEM((nb, 1, width), f32),
            pltpu.VMEM((nb, 1, width), f32),
            pltpu.VMEM((2, length, head), bf),
            pltpu.VMEM((2, length, head), bf),
            pltpu.VMEM((rows, 128), f32),
            dma((2,)),
            dma((DP_CHUNKS, 2)),
            dma((AG_CHUNKS, ntp)),
            dma((AG_CHUNKS, ntp)),
            dma((RS_CHUNKS, ntp)),
            dma((RS_CHUNKS, ntp)),
            dma((DP_CHUNKS, 2 * nd)),
            dma((DP_CHUNKS, 2 * nd)),
            dma((nb,)),
            dma((nb,)),
            dma((2,)),
            dma((2,)),
        ],
        compiler_params=pltpu.CompilerParams(
            collective_id=0, has_side_effects=True, vmem_limit_bytes=48 * 1024 * 1024),
    )(activations, cotangent, segment_ids.reshape(1, length), norm_gain.reshape(1, width),
      jnp.asarray(cosine), jnp.asarray(sine), query_weight, key_value_weight)
    return (outs[0], outs[1], outs[2], outs[3].reshape(width))


def solution(mesh):
    return jax.shard_map(
        functools.partial(on_device, mesh.shape["tp"], mesh.shape["dp"]),
        mesh=mesh,
        in_specs=(P(("dp", "tp"), None), P("dp", "tp"), P("dp"), P(), P(None, "tp"), P(None, "tp")),
        out_specs=(P(("dp", "tp"), None), P(None, "tp"), P(None, "tp"), P()),
        check_vma=False,
    )
```

time: 197 us -> 93.9 us (0.48)
  waiting for transfers between devices: 114 us -> 0 us
  Pallas kernels: 0 us -> 82 us
  blocking collectives: 42.6 us -> 0 us
  matrix products: 13.5 us -> 0 us
  between operations: 13.9 us -> 0.66 us
  other arithmetic: 8.2 us -> 0 us
  local copies, waits for them, and re-layouts: 3.36 us -> 10.9 us
    pallas_call x0 -> x1, Pallas kernels: none -> 82 us  [on_device(): pl.pallas_call(functools.partial(kernel, ntp, ndp), out_shape=[jax.ShapeD...]
    psum x1 -> x0, waiting for transfers between devices: 61.8 us -> none  [on_device(): lax.psum(query_term.astype(jnp.bfloat16), 'dp').astype(jnp.float32)]
    psum x1 -> x0, blocking collectives: 42.6 us -> none  [on_device(): gain_grad = lax.psum(gain_term, ('dp', 'tp'))]
    reduce_scatter x1 -> x0, waiting for transfers between devices: 27.2 us -> none  [on_device(): lax.psum_scatter((total + times_transposed(incoming, key_value_weight)).a...]
    all_gather x1 -> x0, waiting for transfers between devices: 25.4 us -> none  [on_device(): normed = lax.all_gather(normed_local, 'tp', axis=0, tiled=True)]
    dot_general x13 -> x0, matrix products: 13.5 us -> none  [the longest x5 4.68 us: contract_rows(): lax.dot_general(left, right, (((0,), (0,)), ((), ())), preferred_element_...]
    unnamed x18 -> x20, local copies, waits for them, and re-layouts: 3.36 us -> 10.9 us
    convert_element_type x4 -> x0, other arithmetic: 4.29 us -> none  [the longest x1 2.13 us: on_device(): input_grad = ((scaled - unit_rows * inner) / root_mean).astype(jnp.bfloat16)]
  transfers between devices with their start and end apart: 5 -> 0, of which waited for: 3 -> 0; matrix products, arithmetic and copies ran while one was open for 6% -> 0% of each run, Pallas kernels for 0% -> 0%
where the time goes in v1:
time: 93.9 us; the launch traced here: 93.5 us
  Pallas kernels  82 us (87%)
  local copies, waits for them, and re-layouts  10.9 us (12%)
    pallas_call x1, Pallas kernels, on_device(): pl.pallas_call(functools.partial(kernel, ntp, ndp), out_shape=[jax.ShapeD...  82 us
    unnamed x20, local copies, waits for them, and re-layouts  10.9 us

profile of v1, /device:TPU:0, one launch (start us, length us, event | category | flops | bytes accessed | tf_op | source)
XLA Modules:
  0.0 93.5 jit_solution(13810724500170710420)
XLA Ops:
  0.6 0.0 copy-start.7
  0.6 0.7 copy-done.7
  1.3 0.0 copy-start
  1.3 1.2 %copy-done = bf16[4096,128]{1,0:T(8,128)(2,1)S(1)} copy-done((bf16[4096,128]{1,0:T(8,128)(2,1)S(1)}, bf16[4096,128]{1,0:T(8,128)(2,1)}, u32[]{:S(2)}) %copy-start) | copy-done | bytes 1048600
  2.5 0.0 copy-start.1
  2.5 1.2 %copy-done.1 = bf16[4096,128]{1,0:T(8,128)(2,1)S(1)} copy-done((bf16[4096,128]{1,0:T(8,128)(2,1)S(1)}, bf16[4096,128]{1,0:T(8,128)(2,1)}, u32[]{:S(2)}) %copy-start.1) | copy-done | bytes 1048600
  3.8 0.0 copy-start.2
  3.8 1.0 %copy-done.2 = bf16[64,4096]{1,0:T(8,128)(2,1)S(1)} copy-done((bf16[64,4096]{1,0:T(8,128)(2,1)S(1)}, bf16[64,4096]{1,0:T(8,128)(2,1)}, u32[]{:S(2)}) %copy-start.2) | copy-done | bytes 524312
  4.8 0.0 copy-start.3
  4.8 0.9 copy-done.3
  5.7 0.0 copy-start.4
  5.7 0.9 copy-done.4
  6.6 0.0 copy-start.5
  6.6 0.8 copy-done.5
  7.5 0.0 copy-start.6
  7.5 0.7 copy-done.6
  8.2 82.0 %shard_map.111 = (bf16[64,4096]{1,0:T(8,128)(2,1)S(1)}, bf16[4096,128]{1,0:T(8,128)(2,1)S(1)}, bf16[4096,128]{1,0:T(8,128)(2,1)S(1)}, f32[1,4096]{1,0:T(1,128)S(1)}) custom-call(bf16[64,4096]{1,0:T(8,128)(2,1)S(1)} %copy-done.2, bf16[256,128]{1,0:T(8,128)(2,1)S(1)} %copy-done.5, s32[1,256]{1,0:T(1,128)S(1)} %bitcast.5, f32[1,4096]{1,0:T(1,128)S(1)} %bitcast.3, ...), custom_call_target="tpu_custom_call" | custom-call | tf_op jit(solution)/shard_map/pallas_call | solution.py:303
  90.2 0.8 copy.16
  91.0 1.0 %copy.17 = bf16[4096,128]{1,0:T(8,128)(2,1)} copy(bf16[4096,128]{1,0:T(8,128)(2,1)S(1)} %get-tuple-element.17) | data formatting | bytes 2097152
  92.0 1.0 %copy.18 = bf16[4096,128]{1,0:T(8,128)(2,1)} copy(bf16[4096,128]{1,0:T(8,128)(2,1)S(1)} %get-tuple-element.18) | data formatting | bytes 2097152
  92.9 0.6 copy.19
Async XLA Ops:
  0.6 0.7 copy-start.7
  1.3 1.2 %copy-start = (bf16[4096,128]{1,0:T(8,128)(2,1)S(1)}, bf16[4096,128]{1,0:T(8,128)(2,1)}, u32[]{:S(2)}) copy-start(bf16[4096,128]{1,0:T(8,128)(2,1)} %wq_ref.1) | copy-start | bytes 3145732
  2.5 1.2 %copy-start.1 = (bf16[4096,128]{1,0:T(8,128)(2,1)S(1)}, bf16[4096,128]{1,0:T(8,128)(2,1)}, u32[]{:S(2)}) copy-start(bf16[4096,128]{1,0:T(8,128)(2,1)} %wkv_ref.1) | copy-start | bytes 3145732
  3.8 1.0 %copy-start.2 = (bf16[64,4096]{1,0:T(8,128)(2,1)S(1)}, bf16[64,4096]{1,0:T(8,128)(2,1)}, u32[]{:S(2)}) copy-start(bf16[64,4096]{1,0:T(8,128)(2,1)} %x_ref.1) | copy-start | bytes 1572868
  4.8 0.9 copy-start.3
  5.7 0.9 copy-start.4
  6.6 0.8 copy-start.5
  7.5 0.7 copy-start.6

commit v2 on v1

--- a/solution.py
+++ b/solution.py
@@ -10,7 +10,7 @@
 
 EPS = 1e-05
 AG_CHUNKS = 4
-DP_CHUNKS = 4
+DP_CHUNKS = 8
 RS_CHUNKS = 4
 
 
@@ -40,20 +40,31 @@
 
 def kernel(ntp, ndp, x_ref, cot_ref, seg_ref, gain_ref, cos_ref, sin_ref, wq_ref, wkv_ref,
            ig_ref, qg_ref, kvg_ref, gg_ref,
-           wcat, normed, grads, tot, rs_out, rs_in, term, halves, whole, gs, gr, kv_out, kv_in, inv_ref,
-           w_sem, o_sem, ag_s, ag_r, rs_s, rs_r, dp_s, dp_r, g_s, g_r, kv_s, kv_r):
+           wcat, normed, normed_x, grads, grads_x, tot, rs_out, rs_in, term, chain, whole, gs, gr,
+           kv_out, kv_in, inv_ref,
+           w_sem, o_sem, ag_s, ag_r, nx_s, nx_r, gx_s, gx_r, rs_s, rs_r, in_s, in_r, down_s, down_r,
+           last_s, last_r, g_s, g_r, kv_s, kv_r):
     tp, dp = lax.axis_index("tp"), lax.axis_index("dp")
     tp_bits, dp_bits = bits_of(ntp), bits_of(ndp)
     rows, width = x_ref.shape
     length = cot_ref.shape[0]
     head = cot_ref.shape[1]
     sends = []
-
-    def remote(src, dst, s, r, axis, b):
-        me = tp if axis == "tp" else dp
+    x, z, deep = lax.rem(dp, 2), lax.div(dp, 2), ndp // 2
+    middle = deep // 2 - 1
+    side = lax.div(z, deep // 2)
+    depth = z + side * (deep - 1 - 2 * z)
+    inner_dp = dp + 2 * (1 - 2 * side)
+    outer_dp = dp - 2 * (1 - 2 * side)
+    is_middle = lax.div(depth, middle) if middle else 1
+
+    def to(src, dst, s, r, axis, device):
         return pltpu.make_async_remote_copy(
             src_ref=src, dst_ref=dst, send_sem=s, recv_sem=r,
-            device_id={axis: xor(me, b)}, device_id_type=pl.DeviceIdType.MESH)
+            device_id={axis: device}, device_id_type=pl.DeviceIdType.MESH)
+
+    def remote(src, dst, s, r, axis, b):
+        return to(src, dst, s, r, axis, xor(tp if axis == "tp" else dp, b))
 
     def go(copy):
         copy.start()
@@ -67,6 +78,10 @@
         pl.semaphore_signal(barrier, inc=1, device_id={"dp": xor(dp, b)},
                             device_id_type=pl.DeviceIdType.MESH)
 
+    for step in (2, ndp - 2):
+        pl.semaphore_signal(barrier, inc=1, device_id={"dp": lax.rem(dp + step, ndp)},
+                            device_id_type=pl.DeviceIdType.MESH)
+
     w_copies = [pltpu.make_async_copy(wq_ref, wcat.at[:, 0:head], w_sem.at[0]),
                 pltpu.make_async_copy(wkv_ref, wcat.at[:, head:2 * head], w_sem.at[1])]
     for copy in w_copies:
@@ -87,19 +102,35 @@
     inv = 1.0 / jnp.sqrt(square * (1.0 / width) + EPS)
     inv_ref[...] = jnp.broadcast_to(inv, inv_ref.shape)
 
+    half = width // 2
+    held = AG_CHUNKS // 2
+
+    def turn(c):
+        at = lax.rem(c + held * (1 - x), AG_CHUNKS) * cw
+        return pl.ds(pl.multiple_of(at, cw), cw)
+
+    def nx(c, d):
+        if d & 1:
+            part = normed_x.at[block(d ^ 1), cols(c)]
+            return remote(part, part, nx_s.at[c, d], nx_r.at[c, d], "tp", 1)
+        return remote(normed.at[block(d), turn(c)], normed_x.at[block(d), cols(c)],
+                      nx_s.at[c, d], nx_r.at[c, d], "dp", 1)
+
     def ag(c, d):
         b = low_bit(d)
-        part = normed.at[block(d ^ b), cols(c)]
+        part = normed.at[block(d ^ b), turn(c)]
         return remote(part, part, ag_s.at[c, d], ag_r.at[c, d], "tp", b)
 
     order = sorted(range(1, ntp), key=lambda d: -low_bit(d))
     for c in range(AG_CHUNKS):
-        unit = x_ref[:, cols(c)].astype(jnp.float32) * inv
-        normed[block(0), cols(c)] = (unit * gain_ref[:, cols(c)]).astype(jnp.bfloat16)
+        unit = x_ref[:, turn(c)].astype(jnp.float32) * inv
+        normed[block(0), turn(c)] = (unit * gain_ref[:, turn(c)]).astype(jnp.bfloat16)
         if c == 0:
-            pl.semaphore_wait(barrier, len(tp_bits) + len(dp_bits))
+            pl.semaphore_wait(barrier, len(tp_bits) + len(dp_bits) + 2)
         for b in reversed(tp_bits):
             go(ag(c, b))
+        if c < held:
+            go(nx(c, 0))
     for copy in w_copies:
         copy.wait()
     proj = jnp.zeros((length, 2 * head), jnp.float32)
@@ -111,17 +142,24 @@
                 for b in reversed(tp_bits):
                     if b < low_bit(d):
                         go(ag(c, d | b))
+                if c < held:
+                    go(nx(c, d))
 
     def arrive(c, proj):
         for d in order:
             if low_bit(d) == 1:
                 ag(c, d).wait_recv()
-        return proj + dot(normed[:, cols(c)], wcat[cols(c), :], 1, 0)
+        return proj + dot(normed[:, turn(c)], wcat[turn(c), :], 1, 0)
 
     forward(0)
     for c in range(AG_CHUNKS):
         if c + 1 < AG_CHUNKS:
             forward(c + 1)
+        if c == AG_CHUNKS - 1:
+            for i in range(held):
+                for d in range(0, ntp, 2):
+                    nx(i, d).wait_recv()
+                    go(nx(i, d | 1))
         proj = arrive(c, proj)
 
     odd = lax.rem(tp, 2) == 1
@@ -167,46 +205,79 @@
     swap.wait_recv()
     grads[:, head:] = (own_grad + kv_in[1].astype(jnp.float32)).astype(jnp.bfloat16)
 
+    send_grads = remote(grads, grads_x, gx_s, gx_r, "dp", 1)
+    go(send_grads)
+
     local = []
-
-    def dp_task(q):
-        bits = dp_bits if q % 2 == 0 else dp_bits[1:] + dp_bits[:1]
-        nb = len(bits)
-        size = width // DP_CHUNKS
-        term[cols(q, size), :] = dot(normed[:, cols(q, size)], grads[...], 0, 0).astype(jnp.bfloat16)
-        start, count, offset = q * size, size, 0
-        starts = []
-        copies = []
-        for k, b in enumerate(bits):
-            count = count // 2
-            up = bit_at(dp, b)
-            starts.append(start)
-            away = pl.multiple_of(start + (1 - up) * count, count)
-            keep = pl.multiple_of(start + up * count, count)
-            land = halves.at[q, pl.ds(offset, count), :]
-            copy = remote(term.at[pl.ds(away, count), :], land, dp_s.at[q, k], dp_r.at[q, k], "dp", b)
-            go(copy)
-            yield
-            copy.wait_recv()
-            summed = (term[pl.ds(keep, count), :].astype(jnp.float32)
-                      + halves[q, pl.ds(offset, count), :].astype(jnp.float32)).astype(jnp.bfloat16)
-            if k + 1 < nb:
-                term[pl.ds(keep, count), :] = summed
-            else:
-                whole[pl.ds(keep, count), :] = summed
-            start, offset = keep, offset + count
-        for k in reversed(range(nb)):
-            part = whole.at[pl.ds(start, count), :]
-            copy = remote(part, part, dp_s.at[q, nb + k], dp_r.at[q, nb + k], "dp", bits[k])
-            go(copy)
-            yield
-            copy.wait_recv()
-            start, count = starts[k], count * 2
+    size = half // DP_CHUNKS
+
+    def mine_rows(q):
+        return pl.ds(pl.multiple_of(x * half + q * size, size), size)
+
+    def other_rows(q):
+        return pl.ds(pl.multiple_of((1 - x) * half + q * size, size), size)
+
+    def inward(q):
+        return to(term.at[cols(q, size), :], chain.at[q, is_middle], in_s.at[q], in_r.at[q, is_middle],
+                  "dp", inner_dp)
+
+    def arrived(q, slot):
+        return to(term.at[cols(q, size), :], chain.at[q, slot], in_s.at[q], in_r.at[q, slot], "dp", inner_dp)
+
+    def outward(q):
+        part = whole.at[mine_rows(q), :]
+        return to(part, part, down_s.at[q], down_r.at[q], "dp", outer_dp)
+
+    def final(q):
+        part = whole.at[mine_rows(q), :]
+        return remote(part, part, last_s.at[q], last_r.at[q], "dp", 1)
+
+    def save(q, upper):
         for i, out in enumerate((qg_ref, kvg_ref)):
+            at = other_rows(q) if upper else mine_rows(q)
             copy = pltpu.make_async_copy(
-                whole.at[cols(q, size), i * head:(i + 1) * head], out.at[cols(q, size), :], o_sem.at[q, i])
+                whole.at[at, i * head:(i + 1) * head], out.at[at, :], o_sem.at[q, 2 * upper + i])
             copy.start()
             local.append(copy)
+
+    def form(q):
+        own = dot(normed[:, mine_rows(q)], grads[...], 0, 0)
+        value = own + dot(normed_x[:, cols(q, size)], grads_x[...], 0, 0)
+        term[cols(q, size), :] = value.astype(jnp.bfloat16)
+
+        @pl.when(depth == 0)
+        def _():
+            inward(q).start()
+
+    def gather(q):
+        @pl.when(depth > 0)
+        def _():
+            arrived(q, 0).wait_recv()
+            term[cols(q, size), :] = (term[cols(q, size), :].astype(jnp.float32)
+                                      + chain[q, 0].astype(jnp.float32)).astype(jnp.bfloat16)
+            inward(q).start()
+
+    def finish(q):
+        @pl.when(depth == middle)
+        def _():
+            arrived(q, 1).wait_recv()
+            whole[mine_rows(q), :] = (term[cols(q, size), :].astype(jnp.float32)
+                                      + chain[q, 1].astype(jnp.float32)).astype(jnp.bfloat16)
+
+        @pl.when(depth < middle)
+        def _():
+            outward(q).wait_recv()
+
+        @pl.when(depth > 0)
+        def _():
+            outward(q).start()
+
+        go(final(q))
+        save(q, 0)
+
+    def end(q):
+        final(q).wait_recv()
+        save(q, 1)
 
     rw = width // RS_CHUNKS
     rs_order = sorted(range(1, ntp), key=low_bit)
@@ -237,6 +308,7 @@
         for c in range(RS_CHUNKS):
             tot[:, cols(c, rw)] = dot(grads[...], wcat[cols(c, rw), :], 1, 1)
             rs_send(c, 1)
+        yield
         for b in tp_bits[1:]:
             for c in range(RS_CHUNKS):
                 rs_wait(c, b // 2)
@@ -272,20 +344,33 @@
             else:
                 gg_ref[...] = gs[k] + gr[k]
 
-    tasks = [dp_task(q) for q in range(DP_CHUNKS)] + [tp_task()]
-    while tasks:
-        alive = []
-        for task in tasks:
-            try:
-                next(task)
-                alive.append(task)
-            except StopIteration:
-                pass
-        tasks = alive
+    task = tp_task()
+    next(task)
+    send_grads.wait_recv()
+    for i in range(held):
+        for d in range(0, ntp, 2):
+            nx(i, d | 1).wait_recv()
+    for q in range(DP_CHUNKS):
+        form(q)
+    next(task)
+    for step in range(DP_CHUNKS + 3):
+        for lag, stage in enumerate((gather, finish, end)):
+            if 0 <= step - lag < DP_CHUNKS:
+                stage(step - lag)
+        next(task, None)
+    for _ in task:
+        pass
     for copy in local:
         copy.wait()
     for copy in sends:
         copy.wait_send()
+    for q in range(DP_CHUNKS):
+        inward(q).wait_send()
+
+    @pl.when(depth > 0)
+    def _():
+        for q in range(DP_CHUNKS):
+            outward(q).wait_send()
 
 
 def on_device(ntp, ndp, activations, cotangent, segment_ids, norm_gain, query_weight, key_value_weight):
@@ -299,7 +384,6 @@
     vmem = pl.BlockSpec(memory_space=pltpu.VMEM)
     anywhere = pl.BlockSpec(memory_space=pl.ANY)
     dma = pltpu.SemaphoreType.DMA
-    nd = len(bits_of(ndp))
     outs = pl.pallas_call(
         functools.partial(kernel, ntp, ndp),
         out_shape=[
@@ -313,12 +397,14 @@
         scratch_shapes=[
             pltpu.VMEM((width, 2 * head), bf),
             pltpu.VMEM((length, width), bf),
+            pltpu.VMEM((length, width // 2), bf),
+            pltpu.VMEM((length, 2 * head), bf),
             pltpu.VMEM((length, 2 * head), bf),
             pltpu.VMEM((length, width), f32),
             pltpu.VMEM((ntp, rows, width), bf),
             pltpu.VMEM((ntp, rows, width), bf),
-            pltpu.VMEM((width, 2 * head), bf),
-            pltpu.VMEM((DP_CHUNKS, width // DP_CHUNKS, 2 * head), bf),
+            pltpu.VMEM((width // 2, 2 * head), bf),
+            pltpu.VMEM((DP_CHUNKS, 2, width // 2 // DP_CHUNKS, 2 * head), bf),
             pltpu.VMEM((width, 2 * head), bf),
             pltpu.VMEM((nb, 1, width), f32),
             pltpu.VMEM((nb, 1, width), f32),
@@ -326,20 +412,28 @@
             pltpu.VMEM((2, length, head), bf),
             pltpu.VMEM((rows, 128), f32),
             dma((2,)),
-            dma((DP_CHUNKS, 2)),
+            dma((DP_CHUNKS, 4)),
             dma((AG_CHUNKS, ntp)),
             dma((AG_CHUNKS, ntp)),
+            dma((AG_CHUNKS // 2, ntp)),
+            dma((AG_CHUNKS // 2, ntp)),
+            dma,
+            dma,
             dma((RS_CHUNKS, ntp)),
             dma((RS_CHUNKS, ntp)),
-            dma((DP_CHUNKS, 2 * nd)),
-            dma((DP_CHUNKS, 2 * nd)),
+            dma((DP_CHUNKS,)),
+            dma((DP_CHUNKS, 2)),
+            dma((DP_CHUNKS,)),
+            dma((DP_CHUNKS,)),
+            dma((DP_CHUNKS,)),
+            dma((DP_CHUNKS,)),
             dma((nb,)),
             dma((nb,)),
             dma((2,)),
             dma((2,)),
         ],
         compiler_params=pltpu.CompilerParams(
-            collective_id=0, has_side_effects=True, vmem_limit_bytes=48 * 1024 * 1024),
+            collective_id=0, has_side_effects=True, vmem_limit_bytes=60 * 1024 * 1024),
     )(activations, cotangent, segment_ids.reshape(1, length), norm_gain.reshape(1, width),
       jnp.asarray(cosine), jnp.asarray(sine), query_weight, key_value_weight)
     return (outs[0], outs[1], outs[2], outs[3].reshape(width))

time: 93.9 us -> 89.4 us (0.952)
  local copies, waits for them, and re-layouts: 10.9 us -> 5.14 us
  Pallas kernels: 82 us -> 83.4 us
    unnamed x20 -> x10, local copies, waits for them, and re-layouts: 10.9 us -> 5.14 us
    pallas_call x1, Pallas kernels: 82 us -> 83.4 us  [on_device(): pl.pallas_call(functools.partial(kernel, ntp, ndp), out_shape=[jax.ShapeD...]
where the time goes in v2:
time: 89.4 us; the launch traced here: 89.1 us
  Pallas kernels  83.4 us (93%)
  local copies, waits for them, and re-layouts  5.14 us (6%)
    pallas_call x1, Pallas kernels, on_device(): pl.pallas_call(functools.partial(kernel, ntp, ndp), out_shape=[jax.ShapeD...  83.4 us
    unnamed x10, local copies, waits for them, and re-layouts  5.14 us

profile of v2, /device:TPU:0, one launch (start us, length us, event | category | flops | bytes accessed | tf_op | source)
XLA Modules:
  0.0 89.1 jit_solution(2602336130379809583)
XLA Ops:
  0.6 83.4 %shard_map.111 = (bf16[64,4096]{1,0:T(8,128)(2,1)}, bf16[4096,128]{1,0:T(8,128)(2,1)}, bf16[4096,128]{1,0:T(8,128)(2,1)}, f32[1,4096]{1,0:T(1,128)}) custom-call(bf16[64,4096]{1,0:T(8,128)(2,1)} %x_ref.1, bf16[256,128]{1,0:T(8,128)(2,1)} %cot_ref.1, s32[1,256]{1,0:T(1,128)} %bitcast.5, f32[1,4096]{1,0:T(1,128)} %bitcast.3, ...), custom_call_target="tpu_custom_call" | custom-call | tf_op jit(solution)/shard_map/pallas_call | solution.py:387
  84.0 0.0 copy-start.1
  84.0 2.0 %copy.16 = bf16[64,4096]{1,0:T(8,128)(2,1)} copy(bf16[64,4096]{1,0:T(8,128)(2,1)} %get-tuple-element.16) | data formatting | bytes 1048576
  86.0 0.0 copy-done.1
  86.0 0.0 copy-start
  86.0 1.0 %copy.17 = bf16[4096,128]{1,0:T(8,128)(2,1)} copy(bf16[4096,128]{1,0:T(8,128)(2,1)S(1)} %copy-done.1) | data formatting | bytes 2097152
  86.9 0.6 copy-done
  87.6 0.0 copy-start.2
  87.6 1.0 %copy.18 = bf16[4096,128]{1,0:T(8,128)(2,1)} copy(bf16[4096,128]{1,0:T(8,128)(2,1)S(1)} %copy-done) | data formatting | bytes 2097152
  88.5 0.0 copy-done.2
  88.5 0.6 copy.19
Async XLA Ops:
  84.0 2.0 %copy-start.1 = (bf16[4096,128]{1,0:T(8,128)(2,1)S(1)}, bf16[4096,128]{1,0:T(8,128)(2,1)}, u32[]{:S(2)}) copy-start(bf16[4096,128]{1,0:T(8,128)(2,1)} %get-tuple-element.17) | copy-start | bytes 3145732
  86.0 1.6 %copy-start = (bf16[4096,128]{1,0:T(8,128)(2,1)S(1)}, bf16[4096,128]{1,0:T(8,128)(2,1)}, u32[]{:S(2)}) copy-start(bf16[4096,128]{1,0:T(8,128)(2,1)} %get-tuple-element.18) | copy-start | bytes 3145732
  87.6 1.0 %copy-start.2 = (f32[1,4096]{1,0:T(1,128)S(1)}, f32[1,4096]{1,0:T(1,128)}, u32[]{:S(2)}) copy-start(f32[1,4096]{1,0:T(1,128)} %get-tuple-element.11) | copy-start | bytes 49156

commit v3 on v2

--- a/solution.py
+++ b/solution.py
@@ -11,6 +11,8 @@
 EPS = 1e-05
 AG_CHUNKS = 4
 DP_CHUNKS = 8
+LAGS = (0, 2, 4)
+TASK_AT = 5
 RS_CHUNKS = 4
 
 
@@ -38,12 +40,13 @@
     return lax.dot_general(a, b, (((ca,), (cb,)), ((), ())), preferred_element_type=jnp.float32)
 
 
-def kernel(ntp, ndp, x_ref, cot_ref, seg_ref, gain_ref, cos_ref, sin_ref, wq_ref, wkv_ref,
+def kernel(ntp, ndp, x_hbm, cot_hbm, seg_hbm, gain_hbm, cos_hbm, sin_hbm, wq_ref, wkv_ref,
            ig_ref, qg_ref, kvg_ref, gg_ref,
            wcat, normed, normed_x, grads, grads_x, tot, rs_out, rs_in, term, chain, whole, gs, gr,
            kv_out, kv_in, inv_ref,
            w_sem, o_sem, ag_s, ag_r, nx_s, nx_r, gx_s, gx_r, rs_s, rs_r, in_s, in_r, down_s, down_r,
-           last_s, last_r, g_s, g_r, kv_s, kv_r):
+           last_s, last_r, g_s, g_r, kv_s, kv_r,
+           x_ref, cot_ref, seg_ref, gain_ref, cos_ref, sin_ref, load_sem):
     tp, dp = lax.axis_index("tp"), lax.axis_index("dp")
     tp_bits, dp_bits = bits_of(ntp), bits_of(ndp)
     rows, width = x_ref.shape
@@ -70,6 +73,11 @@
         copy.start()
         sends.append(copy)
 
+    loads = [pltpu.make_async_copy(src, dst, load_sem.at[i]) for i, (src, dst) in enumerate((
+        (x_hbm, x_ref), (gain_hbm, gain_ref), (cot_hbm, cot_ref), (seg_hbm, seg_ref),
+        (cos_hbm, cos_ref), (sin_hbm, sin_ref)))]
+    for copy in loads:
+        copy.start()
     barrier = pltpu.get_barrier_semaphore()
     for b in tp_bits:
         pl.semaphore_signal(barrier, inc=1, device_id={"tp": xor(tp, b)},
@@ -95,6 +103,8 @@
     def cols(c, w=cw):
         return slice(c * w, (c + 1) * w)
 
+    for copy in loads:
+        copy.wait()
     square = jnp.zeros((rows, 1), jnp.float32)
     for c in range(AG_CHUNKS):
         v = x_ref[:, cols(c)].astype(jnp.float32)
@@ -353,11 +363,12 @@
     for q in range(DP_CHUNKS):
         form(q)
     next(task)
-    for step in range(DP_CHUNKS + 3):
-        for lag, stage in enumerate((gather, finish, end)):
+    for step in range(DP_CHUNKS + LAGS[2]):
+        for lag, stage in zip(LAGS, (gather, finish, end)):
             if 0 <= step - lag < DP_CHUNKS:
                 stage(step - lag)
-        next(task, None)
+        if step >= TASK_AT:
+            next(task, None)
     for _ in task:
         pass
     for copy in local:
@@ -383,6 +394,7 @@
     bf, f32 = jnp.bfloat16, jnp.float32
     vmem = pl.BlockSpec(memory_space=pltpu.VMEM)
     anywhere = pl.BlockSpec(memory_space=pl.ANY)
+    hbm = pl.BlockSpec(memory_space=pltpu.HBM)
     dma = pltpu.SemaphoreType.DMA
     outs = pl.pallas_call(
         functools.partial(kernel, ntp, ndp),
@@ -392,7 +404,7 @@
             jax.ShapeDtypeStruct((width, head), bf),
             jax.ShapeDtypeStruct((1, width), f32),
         ],
-        in_specs=[vmem] * 6 + [anywhere] * 2,
+        in_specs=[hbm] * 8,
         out_specs=[vmem, anywhere, anywhere, vmem],
         scratch_shapes=[
             pltpu.VMEM((width, 2 * head), bf),
@@ -431,6 +443,13 @@
             dma((nb,)),
             dma((2,)),
             dma((2,)),
+            pltpu.VMEM((rows, width), bf),
+            pltpu.VMEM((length, head), bf),
+            pltpu.VMEM((1, length), jnp.int32),
+            pltpu.VMEM((1, width), f32),
+            pltpu.VMEM((length, head), f32),
+            pltpu.VMEM((length, head), f32),
+            dma((6,)),
         ],
         compiler_params=pltpu.CompilerParams(
             collective_id=0, has_side_effects=True, vmem_limit_bytes=60 * 1024 * 1024),

time: 89.4 us -> 77.8 us (0.87)
  Pallas kernels: 83.4 us -> 71.8 us
    pallas_call x1, Pallas kernels: 83.4 us -> 71.8 us  [on_device(): pl.pallas_call(functools.partial(kernel, ntp, ndp), out_shape=[jax.ShapeD...]
where the time goes in v3:
time: 77.8 us; the launch traced here: 77.6 us
  Pallas kernels  71.8 us (92%)
  local copies, waits for them, and re-layouts  5.14 us (7%)
    pallas_call x1, Pallas kernels, on_device(): pl.pallas_call(functools.partial(kernel, ntp, ndp), out_shape=[jax.ShapeD...  71.8 us
    unnamed x10, local copies, waits for them, and re-layouts  5.14 us

profile of v3, /device:TPU:0, one launch (start us, length us, event | category | flops | bytes accessed | tf_op | source)
XLA Modules:
  0.0 77.6 jit_solution(3079394075391040983)
XLA Ops:
  0.6 71.8 %shard_map.111 = (bf16[64,4096]{1,0:T(8,128)(2,1)}, bf16[4096,128]{1,0:T(8,128)(2,1)}, bf16[4096,128]{1,0:T(8,128)(2,1)}, f32[1,4096]{1,0:T(1,128)}) custom-call(bf16[64,4096]{1,0:T(8,128)(2,1)} %x_hbm.1, bf16[256,128]{1,0:T(8,128)(2,1)} %cot_hbm.1, s32[1,256]{1,0:T(1,128)} %bitcast.5, f32[1,4096]{1,0:T(1,128)} %bitcast.3, ...), custom_call_target="tpu_custom_call" | custom-call | tf_op jit(solution)/shard_map/pallas_call | solution.py:399
  72.4 0.0 copy-start.1
  72.4 2.0 %copy.16 = bf16[64,4096]{1,0:T(8,128)(2,1)} copy(bf16[64,4096]{1,0:T(8,128)(2,1)} %get-tuple-element.16) | data formatting | bytes 1048576
  74.4 0.0 copy-done.1
  74.4 0.0 copy-start
  74.4 1.0 %copy.17 = bf16[4096,128]{1,0:T(8,128)(2,1)} copy(bf16[4096,128]{1,0:T(8,128)(2,1)S(1)} %copy-done.1) | data formatting | bytes 2097152
  75.4 0.6 copy-done
  76.0 0.0 copy-start.2
  76.0 1.0 %copy.18 = bf16[4096,128]{1,0:T(8,128)(2,1)} copy(bf16[4096,128]{1,0:T(8,128)(2,1)S(1)} %copy-done) | data formatting | bytes 2097152
  77.0 0.0 copy-done.2
  77.0 0.6 copy.19
Async XLA Ops:
  72.4 2.0 %copy-start.1 = (bf16[4096,128]{1,0:T(8,128)(2,1)S(1)}, bf16[4096,128]{1,0:T(8,128)(2,1)}, u32[]{:S(2)}) copy-start(bf16[4096,128]{1,0:T(8,128)(2,1)} %get-tuple-element.17) | copy-start | bytes 3145732
  74.4 1.6 %copy-start = (bf16[4096,128]{1,0:T(8,128)(2,1)S(1)}, bf16[4096,128]{1,0:T(8,128)(2,1)}, u32[]{:S(2)}) copy-start(bf16[4096,128]{1,0:T(8,128)(2,1)} %get-tuple-element.18) | copy-start | bytes 3145732
  76.0 1.0 %copy-start.2 = (f32[1,4096]{1,0:T(1,128)S(1)}, f32[1,4096]{1,0:T(1,128)}, u32[]{:S(2)}) copy-start(f32[1,4096]{1,0:T(1,128)} %get-tuple-element.11) | copy-start | bytes 49156

commit v4 on v3

--- a/solution.py
+++ b/solution.py
@@ -10,9 +10,9 @@
 
 EPS = 1e-05
 AG_CHUNKS = 4
-DP_CHUNKS = 8
-LAGS = (0, 2, 4)
-TASK_AT = 5
+DP_CHUNKS = 16
+LAGS = (0, 3, 6)
+TASK_AT = 8
 RS_CHUNKS = 4
 
 
@@ -367,7 +367,7 @@
         for lag, stage in zip(LAGS, (gather, finish, end)):
             if 0 <= step - lag < DP_CHUNKS:
                 stage(step - lag)
-        if step >= TASK_AT:
+        if step >= TASK_AT and (step - TASK_AT) % 2 == 0:
             next(task, None)
     for _ in task:
         pass

time: 77.8 us -> 77.3 us (level)
  no operation moved by 1% of the time
where the time goes in v4:
time: 77.3 us; the launch traced here: 77.1 us
  Pallas kernels  71.3 us (92%)
  local copies, waits for them, and re-layouts  5.14 us (7%)
    pallas_call x1, Pallas kernels, on_device(): pl.pallas_call(functools.partial(kernel, ntp, ndp), out_shape=[jax.ShapeD...  71.3 us
    unnamed x10, local copies, waits for them, and re-layouts  5.14 us

profile of v4, /device:TPU:0, one launch (start us, length us, event | category | flops | bytes accessed | tf_op | source)
XLA Modules:
  0.0 77.1 jit_solution(15873621947938760699)
XLA Ops:
  0.6 71.3 %shard_map.111 = (bf16[64,4096]{1,0:T(8,128)(2,1)}, bf16[4096,128]{1,0:T(8,128)(2,1)}, bf16[4096,128]{1,0:T(8,128)(2,1)}, f32[1,4096]{1,0:T(1,128)}) custom-call(bf16[64,4096]{1,0:T(8,128)(2,1)} %x_hbm.1, bf16[256,128]{1,0:T(8,128)(2,1)} %cot_hbm.1, s32[1,256]{1,0:T(1,128)} %bitcast.5, f32[1,4096]{1,0:T(1,128)} %bitcast.3, ...), custom_call_target="tpu_custom_call" | custom-call | tf_op jit(solution)/shard_map/pallas_call | solution.py:399
  71.9 0.0 copy-start.1
  71.9 2.0 %copy.16 = bf16[64,4096]{1,0:T(8,128)(2,1)} copy(bf16[64,4096]{1,0:T(8,128)(2,1)} %get-tuple-element.16) | data formatting | bytes 1048576
  73.9 0.0 copy-done.1
  73.9 0.0 copy-start
  73.9 1.0 %copy.17 = bf16[4096,128]{1,0:T(8,128)(2,1)} copy(bf16[4096,128]{1,0:T(8,128)(2,1)S(1)} %copy-done.1) | data formatting | bytes 2097152
  74.9 0.6 copy-done
  75.5 0.0 copy-start.2
  75.5 1.0 %copy.18 = bf16[4096,128]{1,0:T(8,128)(2,1)} copy(bf16[4096,128]{1,0:T(8,128)(2,1)S(1)} %copy-done) | data formatting | bytes 2097152
  76.5 0.0 copy-done.2
  76.5 0.6 copy.19
Async XLA Ops:
  71.9 2.0 %copy-start.1 = (bf16[4096,128]{1,0:T(8,128)(2,1)S(1)}, bf16[4096,128]{1,0:T(8,128)(2,1)}, u32[]{:S(2)}) copy-start(bf16[4096,128]{1,0:T(8,128)(2,1)} %get-tuple-element.17) | copy-start | bytes 3145732
  73.9 1.6 %copy-start = (bf16[4096,128]{1,0:T(8,128)(2,1)S(1)}, bf16[4096,128]{1,0:T(8,128)(2,1)}, u32[]{:S(2)}) copy-start(bf16[4096,128]{1,0:T(8,128)(2,1)} %get-tuple-element.18) | copy-start | bytes 3145732
  75.5 1.0 %copy-start.2 = (f32[1,4096]{1,0:T(1,128)S(1)}, f32[1,4096]{1,0:T(1,128)}, u32[]{:S(2)}) copy-start(f32[1,4096]{1,0:T(1,128)} %get-tuple-element.11) | copy-start | bytes 49156

commit v5 on v4

--- a/solution.py
+++ b/solution.py
@@ -360,9 +360,11 @@
     for i in range(held):
         for d in range(0, ntp, 2):
             nx(i, d | 1).wait_recv()
-    for q in range(DP_CHUNKS):
+    for q in range(DP_CHUNKS // 2):
         form(q)
     next(task)
+    for q in range(DP_CHUNKS // 2, DP_CHUNKS):
+        form(q)
     for step in range(DP_CHUNKS + LAGS[2]):
         for lag, stage in zip(LAGS, (gather, finish, end)):
             if 0 <= step - lag < DP_CHUNKS:

time: 77.3 us -> 76.9 us (level)
  no operation moved by 1% of the time
where the time goes in v5:
time: 76.9 us; the launch traced here: 76.7 us
  Pallas kernels  70.9 us (92%)
  local copies, waits for them, and re-layouts  5.14 us (7%)
    pallas_call x1, Pallas kernels, on_device(): pl.pallas_call(functools.partial(kernel, ntp, ndp), out_shape=[jax.ShapeD...  70.9 us
    unnamed x10, local copies, waits for them, and re-layouts  5.14 us

profile of v5, /device:TPU:0, one launch (start us, length us, event | category | flops | bytes accessed | tf_op | source)
XLA Modules:
  0.0 76.7 jit_solution(3796830521852895696)
XLA Ops:
  0.6 70.9 %shard_map.111 = (bf16[64,4096]{1,0:T(8,128)(2,1)}, bf16[4096,128]{1,0:T(8,128)(2,1)}, bf16[4096,128]{1,0:T(8,128)(2,1)}, f32[1,4096]{1,0:T(1,128)}) custom-call(bf16[64,4096]{1,0:T(8,128)(2,1)} %x_hbm.1, bf16[256,128]{1,0:T(8,128)(2,1)} %cot_hbm.1, s32[1,256]{1,0:T(1,128)} %bitcast.5, f32[1,4096]{1,0:T(1,128)} %bitcast.3, ...), custom_call_target="tpu_custom_call" | custom-call | tf_op jit(solution)/shard_map/pallas_call | solution.py:401
  71.6 0.0 copy-start.1
  71.6 2.0 %copy.16 = bf16[64,4096]{1,0:T(8,128)(2,1)} copy(bf16[64,4096]{1,0:T(8,128)(2,1)} %get-tuple-element.16) | data formatting | bytes 1048576
  73.5 0.0 copy-done.1
  73.5 0.0 copy-start
  73.5 1.0 %copy.17 = bf16[4096,128]{1,0:T(8,128)(2,1)} copy(bf16[4096,128]{1,0:T(8,128)(2,1)S(1)} %copy-done.1) | data formatting | bytes 2097152
  74.5 0.6 copy-done
  75.1 0.0 copy-start.2
  75.1 1.0 %copy.18 = bf16[4096,128]{1,0:T(8,128)(2,1)} copy(bf16[4096,128]{1,0:T(8,128)(2,1)S(1)} %copy-done) | data formatting | bytes 2097152
  76.1 0.0 copy-done.2
  76.1 0.6 copy.19
Async XLA Ops:
  71.6 2.0 %copy-start.1 = (bf16[4096,128]{1,0:T(8,128)(2,1)S(1)}, bf16[4096,128]{1,0:T(8,128)(2,1)}, u32[]{:S(2)}) copy-start(bf16[4096,128]{1,0:T(8,128)(2,1)} %get-tuple-element.17) | copy-start | bytes 3145732
  73.5 1.6 %copy-start = (bf16[4096,128]{1,0:T(8,128)(2,1)S(1)}, bf16[4096,128]{1,0:T(8,128)(2,1)}, u32[]{:S(2)}) copy-start(bf16[4096,128]{1,0:T(8,128)(2,1)} %get-tuple-element.18) | copy-start | bytes 3145732
  75.1 1.0 %copy-start.2 = (f32[1,4096]{1,0:T(1,128)S(1)}, f32[1,4096]{1,0:T(1,128)}, u32[]{:S(2)}) copy-start(f32[1,4096]{1,0:T(1,128)} %get-tuple-element.11) | copy-start | bytes 49156
